TPU v7x, 32 devices: a whole 2x2x4 slice. The times are simulated.
32 devices in a mesh: space: 8 (over z, x), vel: 4 (over y, core).
Axes of the slice: x: 2, y: 2, z: 4, core: 2. Of those that a mesh axis runs over, the one named last changes fastest.
Arguments:
- probe_field: float32 [2, 1024, 1024], P(None, 'space'), may hold values from -6 to 6
- control_field: float32 [2, 1024, 1024], P(None, 'space'), may hold values from -4 to 4
- optical_state: float32 [2, 64, 1024, 1024], P(None, 'vel', 'space'), may hold values from -3 to 3
- spin_state: float32 [2, 64, 1024, 1024], P(None, 'vel', 'space'), may hold values from -3 to 3
- doppler_shift: float32 [64], P('vel'), may hold values from -3 to 3
- class_weight: float32 [64], P('vel'), may hold values from 0.2 to 2
- gradient_shift: float32 [1024, 1024], P('space'), may hold values from -3 to 3
Outputs:
- probe_out: float32 [2, 1024, 1024], P(None, 'space')
- control_out: float32 [2, 1024, 1024], P(None, 'space')
- optical_out: float32 [2, 64, 1024, 1024], P(None, 'vel', 'space')
- spin_out: float32 [2, 64, 1024, 1024], P(None, 'vel', 'space')
All inputs are finite; a program needn't handle non-finite values.
Results may differ from a plain program's by a relative error of at most 0.000098.
Values sent between devices are 32-bit elements; how exact they have to be, the bound alone decides.
A program may use at most 192 MiB of HBM per device.

v0:
```python
import jax
import jax.numpy as jnp
import numpy as np
from jax import lax
from jax.sharding import PartitionSpec as P

GRID = 1024
VEL = 64
GAMMA = 1.0
DEPHASE = 0.1
DT = 0.25
COUPLE = 2.0
HIGHEST = lax.Precision.HIGHEST


def circulant_tables(grid_width):
    counter = np.arange(grid_width, dtype=np.int32)
    frequency = np.where(counter < grid_width // 2, counter, counter - grid_width)
    angles = (
        np.float32(np.pi)
        * (frequency * frequency % (2 * grid_width)).astype(np.float32)
        / np.float32(grid_width)
    )
    turns = counter[:, None] * counter[None, :] % grid_width
    argument = (
        np.float32(2.0 * np.pi) * turns.astype(np.float32) / np.float32(grid_width)
        - angles[None, :]
    )
    kernel_real = np.mean(np.cos(argument), axis=1)
    kernel_imag = np.mean(np.sin(argument), axis=1)
    offsets = (counter[:, None] - counter[None, :]) % grid_width
    return (kernel_real[offsets].astype(np.float32), kernel_imag[offsets].astype(np.float32))


def mix_left(table_real, table_imag, section):
    real_in, imag_in = (section[:, 0], section[:, 1])

    def product_of(table, values):
        return jnp.einsum("mn,fnk->fmk", table, values, precision=HIGHEST)

    return jnp.stack(
        [
            product_of(table_real, real_in) - product_of(table_imag, imag_in),
            product_of(table_real, imag_in) + product_of(table_imag, real_in),
        ],
        axis=1,
    )


def mix_right(section, table_real, table_imag):
    real_in, imag_in = (section[:, 0], section[:, 1])

    def product_of(values, table):
        return jnp.einsum("fmn,nk->fmk", values, table, precision=HIGHEST)

    return jnp.stack(
        [
            product_of(real_in, table_real) - product_of(imag_in, table_imag),
            product_of(imag_in, table_real) + product_of(real_in, table_imag),
        ],
        axis=1,
    )


def derivative(optical, spin_part, probe_part, control, doppler, gradient):
    optical_real, optical_imag = (optical[0], optical[1])
    spin_real, spin_imag = (spin_part[0], spin_part[1])
    probe_real, probe_imag = (probe_part[0], probe_part[1])
    control_real, control_imag = (control[0], control[1])
    rate_optical_real = (
        -GAMMA * optical_real
        + doppler * optical_imag
        - probe_imag
        - (control_real * spin_imag + control_imag * spin_real)
    )
    rate_optical_imag = (
        -GAMMA * optical_imag
        - doppler * optical_real
        + probe_real
        + (control_real * spin_real - control_imag * spin_imag)
    )
    rate_spin_real = (
        -DEPHASE * spin_real
        + gradient * spin_imag
        - (control_real * optical_imag - control_imag * optical_real)
    )
    rate_spin_imag = (
        -DEPHASE * spin_imag
        - gradient * spin_real
        + (control_real * optical_real + control_imag * optical_imag)
    )
    return (
        jnp.stack([rate_optical_real, rate_optical_imag]),
        jnp.stack([rate_spin_real, rate_spin_imag]),
    )


def midpoint(optical, spin_part, probe_part, control, doppler, gradient):
    rate_optical, rate_spin = derivative(optical, spin_part, probe_part, control, doppler, gradient)
    half_optical = optical + 0.5 * DT * rate_optical
    half_spin = spin_part + 0.5 * DT * rate_spin
    rate_optical, rate_spin = derivative(
        half_optical, half_spin, probe_part, control, doppler, gradient
    )
    return (optical + DT * rate_optical, spin_part + DT * rate_spin)


def add_source(complex_field, polarization):
    return jnp.stack(
        [complex_field[0] - COUPLE * polarization[1], complex_field[1] + COUPLE * polarization[0]]
    )


def shards(
    probe_field,
    control_field,
    optical_state,
    spin_state,
    doppler_shift,
    class_weight,
    gradient_shift,
):
    grid_width = GRID
    quarter_width = grid_width // lax.axis_size("vel")
    table_real, table_imag = circulant_tables(grid_width)
    full_real = jnp.asarray(table_real)
    full_imag = jnp.asarray(table_imag)

    def row_mix(section):
        blended = mix_left(
            full_real,
            full_imag,
            lax.all_to_all(section, "space", split_axis=3, concat_axis=2, tiled=True),
        )
        return lax.all_to_all(blended, "space", split_axis=2, concat_axis=3, tiled=True)

    def spread(section):
        return lax.all_gather(section, "vel", axis=3, tiled=True)

    stacked = jnp.stack([probe_field, control_field])
    col_start = lax.axis_index("vel") * quarter_width
    quart_real = lax.dynamic_slice_in_dim(full_real, col_start, quarter_width, 1)
    quart_imag = lax.dynamic_slice_in_dim(full_imag, col_start, quarter_width, 1)
    stacked = spread(row_mix(mix_right(stacked, quart_real, quart_imag)))
    optical_new, spin_new = midpoint(
        optical_state,
        spin_state,
        stacked[0],
        stacked[1],
        doppler_shift[:, None, None],
        gradient_shift,
    )
    weighted = jnp.einsum("cvrn,v->crn", optical_new, class_weight, precision=HIGHEST) / VEL
    polarization = lax.psum_scatter(weighted, "vel", scatter_dimension=2, tiled=True)
    probe_part = lax.dynamic_slice_in_dim(stacked[0], col_start, quarter_width, 2)
    control_part = lax.dynamic_slice_in_dim(stacked[1], col_start, quarter_width, 2)
    section = jnp.stack([add_source(probe_part, polarization), control_part])
    stacked = mix_right(spread(row_mix(section)), full_real, full_imag)
    return (stacked[0], stacked[1], optical_new, spin_new)


def solution(mesh):
    return jax.shard_map(
        shards,
        mesh=mesh,
        in_specs=(
            P(None, "space", None),
            P(None, "space", None),
            P(None, "vel", "space", None),
            P(None, "vel", "space", None),
            P("vel"),
            P("vel"),
            P("space", None),
        ),
        out_specs=(
            P(None, "space", None),
            P(None, "space", None),
            P(None, "vel", "space", None),
            P(None, "vel", "space", None),
        ),
        check_vma=False,
    )
```

profile of v0, /device:TPU:0, one launch (start us, length us, event | category | flops | bytes accessed | tf_op | source)
XLA Modules:
  0.0 411.2 jit_solution(229504936186904210)
XLA Ops:
  17.8 21.6 %all_to_all.72 = f32[2,2,128,256]{2,0,1,3:T(2,128)S(1)} all-to-all(f32[2,2,128,256]{2,0,1,3:T(2,128)S(1)} %copy.38), channel_id=1, replica_groups=mesh['space'=8,'vel'=4] {'space'}, dimensions={3} | all-to-all | bytes 1048576 | tf_op jit(solution)/shard_map/all_to_all | solution.py:133
  39.9 6.4 %fusion.35 = f32[2,32,1024]{2,1,0:T(8,128)S(1)} fusion(f32[1024,1024,1]{1,0,2:T(8,128)} %constant.31, f32[2,2,1024,32]{2,3,0,1:T(8,128)S(1)} %all_to_all.55), kind=kOutput, calls=%fused_computation.75 | convolution fusion | flops 805306368 | bytes 4718592 | tf_op jit(solution)/shard_map/mn,fnk->fmk/dot_general | solution.py:39
  46.3 6.3 %fusion.34 = f32[2,32,1024]{2,1,0:T(8,128)S(1)} fusion(f32[1024,1024,1]{1,0,2:T(8,128)} %constant.31, f32[2,2,1024,32]{2,3,0,1:T(8,128)S(1)} %all_to_all.55), kind=kOutput, calls=%fused_computation.74 | convolution fusion | flops 805306368 | bytes 4718592 | tf_op jit(solution)/shard_map/mn,fnk->fmk/dot_general | solution.py:39
  52.5 4.1 %fusion.10 = f32[2,1,1024,32]{2,3,0,1:T(8,128)S(1)} fusion(f32[2,32,1024]{2,1,0:T(8,128)S(1)} %fusion.35, f32[1024,1024,1]{1,0,2:T(8,128)S(1)} %copy-done.1, f32[2,2,1024,32]{2,3,0,1:T(8,128)S(1)} %all_to_all.55), kind=kOutput, calls=%fused_computation.31 | convolution fusion | flops 805371904 | bytes 4980736 | tf_op jit(solution)/shard_map/mn,fnk->fmk/dot_general | solution.py:39
  56.6 4.6 %fusion.11 = f32[2,1,1024,32]{2,3,0,1:T(8,128)S(1)} fusion(f32[2,32,1024]{2,1,0:T(8,128)S(1)} %fusion.34, f32[1024,1024,1]{1,0,2:T(8,128)S(1)} %copy-done.1, f32[2,2,1024,32]{2,3,0,1:T(8,128)S(1)} %all_to_all.55), kind=kOutput, calls=%fused_computation.33 | convolution fusion | flops 805371904 | bytes 4980736 | tf_op jit(solution)/shard_map/mn,fnk->fmk/dot_general | solution.py:39
  64.8 17.7 %all_to_all.73 = f32[8,1,16384]{2,1,0:T(1,128)S(1)} all-to-all(f32[8,1,16384]{2,1,0:T(1,128)S(1)} %reshape.33), channel_id=1, replica_groups=mesh['space'=8,'vel'=4] {'space'}, dimensions={0} | all-to-all | bytes 1048576 | tf_op jit(solution)/shard_map/all_to_all | solution.py:135
  89.3 21.7 %all-gather.3.cloned.1.call-done = f32[2,2,128,1024]{2,3,1,0:T(8,128)} async-done(((f32[2,2,128,256]{2,3,1,0:T(8,128)}), f32[2,2,128,1024]{2,3,1,0:T(8,128)}) %all-gather.3.cloned.1.call-update) | async-done | bytes 2097168 | tf_op jit(solution)/shard_map/all_gather | solution.py:138
  113.5 18.6 %subtract_subtract_fusion.1 = (f32[1,16,128,1024]{3,2,1,0:T(8,128)}, f32[1,16,128,1024]{3,2,1,0:T(8,128)}) fusion(f32[2,16,128,1024]{3,2,1,0:T(8,128)} %param.12, f32[2,16,128,1024]{3,2,1,0:T(8,128)} %param.11, f32[128,1024]{1,0:T(8,128)S(1)} %copy-done.9, f32[128,1024]{1,0:T(8,128)S(1)} %copy.46, f32[128,1024]{1,0:T(8,128)S(1)} %copy.45), kind=kLoop, calls=%fused_computation.15 | loop fusion | flops 29360128 | bytes 51904512 | tf_op jit(solution)/shard_map/sub | solution.py:83
  132.1 18.4 %add_subtract_fusion.1 = (f32[1,16,128,1024]{3,2,1,0:T(8,128)}, f32[1,16,128,1024]{3,2,1,0:T(8,128)}) fusion(f32[2,16,128,1024]{3,2,1,0:T(8,128)} %param.12, f32[2,16,128,1024]{3,2,1,0:T(8,128)} %param.11, f32[128,1024]{1,0:T(8,128)S(1)} %copy.46, f32[128,1024]{1,0:T(8,128)S(1)} %copy.45, f32[128,1024]{1,0:T(8,128)S(1)} %copy.44, f32[16]{0:T(128)S(1)} %copy-done.10, ...), kind=kLoop, calls=%fused_computation.17 | loop fusion | flops 33554432 | bytes 52428864 | tf_op jit(solution)/shard_map/sub | solution.py:71
  150.5 33.9 %fusion = (f32[2,16,128,1024]{3,2,1,0:T(8,128)}, f32[2,16,128,1024]{3,2,1,0:T(8,128)}) fusion(f32[2,16,128,1024]{3,2,1,0:T(8,128)} %param.11, f32[1,16,128,1024]{3,2,1,0:T(8,128)} %get-tuple-element.11, f32[1,16,128,1024]{3,2,1,0:T(8,128)} %get-tuple-element.10, f32[2,16,128,1024]{3,2,1,0:T(8,128)} %param.12, f32[1,16,128,1024]{3,2,1,0:T(8,128)} %get-tuple-element.7, ...), kind=kLoop, calls=%fused_computation.1 | loop fusion | flops 25165824 | bytes 100663296 | tf_op jit(solution)/shard_map/add | solution.py:100
  184.4 18.4 %add_subtract_fusion = (f32[1,16,128,1024]{3,2,1,0:T(8,128)}, f32[1,16,128,1024]{3,2,1,0:T(8,128)}) fusion(f32[2,16,128,1024]{3,2,1,0:T(8,128)} %get-tuple-element.23, f32[2,16,128,1024]{3,2,1,0:T(8,128)} %get-tuple-element.22, f32[128,1024]{1,0:T(8,128)S(1)} %copy.46, f32[128,1024]{1,0:T(8,128)S(1)} %copy.45, f32[128,1024]{1,0:T(8,128)S(1)} %copy.44, ...), kind=kLoop, calls=%fused_computation.13 | loop fusion | flops 33554432 | bytes 52428864 | tf_op jit(solution)/shard_map/sub | solution.py:71
  202.7 11.9 %fusion.2 = f32[2,16,128,1024]{3,2,1,0:T(8,128)S(1)} fusion(f32[2,16,128,1024]{3,2,1,0:T(8,128)} %param.11, f32[1,16,128,1024]{3,2,1,0:T(8,128)} %get-tuple-element.9, f32[1,16,128,1024]{3,2,1,0:T(8,128)} %get-tuple-element.8), kind=kLoop, calls=%fused_computation.5 | loop fusion | flops 12582912 | bytes 50331648 | tf_op jit(solution)/shard_map/add | solution.py:105
  214.6 6.2 %copy-done.4 = f32[2,16,128,1024]{3,2,1,0:T(8,128)} copy-done((f32[2,16,128,1024]{3,2,1,0:T(8,128)}, f32[2,16,128,1024]{3,2,1,0:T(8,128)S(1)}, u32[]{:S(2)}) %copy-start.4) | copy-done | bytes 16777240
  220.8 16.7 %fusion.4 = f32[1,2,128,1024]{3,0,2,1:T(1,128)} fusion(f32[2,16,128,1024]{3,2,1,0:T(8,128)S(1)} %fusion.2, f32[16]{0:T(128)S(1)} %copy-done), kind=kOutput, calls=%fused_computation.8 | convolution fusion | flops 50331648 | bytes 17825856 | tf_op jit(solution)/shard_map/cvrn,v->crn/dot_general | solution.py:153
  237.5 3.6 copy.57
  244.6 23.8 %reduce-scatter.2.cloned.1.call-done = f32[2,128,256]{1,2,0:T(8,128)} async-done(((f32[2,128,1024]{1,2,0:T(8,128)}), f32[2,128,256]{1,2,0:T(8,128)}) %reduce-scatter.2.cloned.1.call-update) | async-done | bytes 262160 | tf_op jit(solution)/shard_map/reduce_scatter | solution.py:154
  270.0 19.7 %all_to_all.74 = f32[2,2,128,256]{2,1,0,3:T(2,128)S(1)} all-to-all(f32[2,2,128,256]{2,1,0,3:T(2,128)S(1)} %copy.48), channel_id=1, replica_groups=mesh['space'=8,'vel'=4] {'space'}, dimensions={3} | all-to-all | bytes 1048576 | tf_op jit(solution)/shard_map/all_to_all | solution.py:133
  290.1 6.4 %fusion.37 = f32[2,32,1024]{2,1,0:T(8,128)S(1)} fusion(f32[1024,1024,1]{1,0,2:T(8,128)} %constant.31, f32[2,2,1024,32]{2,3,0,1:T(8,128)S(1)} %all_to_all.63), kind=kOutput, calls=%fused_computation.77 | convolution fusion | flops 805306368 | bytes 4718592 | tf_op jit(solution)/shard_map/mn,fnk->fmk/dot_general | solution.py:39
  296.5 6.3 %fusion.36 = f32[2,32,1024]{2,1,0:T(8,128)S(1)} fusion(f32[1024,1024,1]{1,0,2:T(8,128)} %constant.31, f32[2,2,1024,32]{2,3,0,1:T(8,128)S(1)} %all_to_all.63), kind=kOutput, calls=%fused_computation.76 | convolution fusion | flops 805306368 | bytes 4718592 | tf_op jit(solution)/shard_map/mn,fnk->fmk/dot_general | solution.py:39
  302.7 4.1 %fusion.8 = f32[2,1,1024,32]{2,3,0,1:T(8,128)S(1)} fusion(f32[2,32,1024]{2,1,0:T(8,128)S(1)} %fusion.37, f32[1024,1024,1]{1,0,2:T(8,128)S(1)} %copy-done.2, f32[2,2,1024,32]{2,3,0,1:T(8,128)S(1)} %all_to_all.63), kind=kOutput, calls=%fused_computation.27 | convolution fusion | flops 805371904 | bytes 4980736 | tf_op jit(solution)/shard_map/mn,fnk->fmk/dot_general | solution.py:39
  306.9 4.3 %fusion.9 = f32[2,1,1024,32]{2,3,0,1:T(8,128)S(1)} fusion(f32[2,32,1024]{2,1,0:T(8,128)S(1)} %fusion.36, f32[1024,1024,1]{1,0,2:T(8,128)S(1)} %copy-done.2, f32[2,2,1024,32]{2,3,0,1:T(8,128)S(1)} %all_to_all.63), kind=kOutput, calls=%fused_computation.29 | convolution fusion | flops 805371904 | bytes 4980736 | tf_op jit(solution)/shard_map/mn,fnk->fmk/dot_general | solution.py:39
  312.0 2.8 copy.51
  314.8 2.9 reshape.35
  317.7 17.7 %all_to_all.75 = f32[8,1,16384]{2,1,0:T(1,128)S(1)} all-to-all(f32[8,1,16384]{2,1,0:T(1,128)} %reshape.35), channel_id=1, replica_groups=mesh['space'=8,'vel'=4] {'space'}, dimensions={0} | all-to-all | bytes 1048576 | tf_op jit(solution)/shard_map/all_to_all | solution.py:135
  335.4 2.9 reduce.1
  338.3 2.8 reshape.36
  345.5 20.3 %subtract_subtract_fusion = (f32[1,16,128,1024]{3,2,1,0:T(8,128)}, f32[1,16,128,1024]{3,2,1,0:T(8,128)}) fusion(f32[2,16,128,1024]{3,2,1,0:T(8,128)} %get-tuple-element.23, f32[2,16,128,1024]{3,2,1,0:T(8,128)} %get-tuple-element.22, f32[128,1024]{1,0:T(8,128)} %param.15, f32[128,1024]{1,0:T(8,128)S(1)} %copy.46, f32[128,1024]{1,0:T(8,128)S(1)} %copy.45), kind=kLoop, calls=%fused_computation.11 | loop fusion | flops 29360128 | bytes 51904512 | tf_op jit(solution)/shard_map/sub | solution.py:83
  365.8 17.2 %fusion.3 = f32[2,16,128,1024]{3,2,1,0:T(8,128)} fusion(f32[2,16,128,1024]{3,2,1,0:T(8,128)} %param.12, f32[1,16,128,1024]{3,2,1,0:T(8,128)} %get-tuple-element.5, f32[1,16,128,1024]{3,2,1,0:T(8,128)} %get-tuple-element.4), kind=kLoop, calls=%fused_computation.7 | loop fusion | flops 12582912 | bytes 50331648 | tf_op jit(solution)/shard_map/add | solution.py:105
  383.1 6.2 %fusion.31 = f32[2,128,1024]{2,1,0:T(8,128)S(1)} fusion(f32[1024,1024,1]{1,0,2:T(8,128)} %constant.31, f32[2,2,128,1024]{3,2,0,1:T(8,128)} %all-gather.5.cloned.1.call-done), kind=kOutput, calls=%fused_computation.60 | convolution fusion | flops 3221225472 | bytes 6291456 | tf_op jit(solution)/shard_map/fmn,nk->fmk/dot_general | solution.py:54
  389.2 6.2 %fusion.30 = f32[2,128,1024]{2,1,0:T(8,128)S(1)} fusion(f32[1024,1024,1]{1,0,2:T(8,128)} %constant.31, f32[2,2,128,1024]{3,2,0,1:T(8,128)} %all-gather.5.cloned.1.call-done), kind=kOutput, calls=%fused_computation.59 | convolution fusion | flops 3221225472 | bytes 6291456 | tf_op jit(solution)/shard_map/fmn,nk->fmk/dot_general | solution.py:54
  395.5 3.7 fusion.6
  399.2 3.7 fusion.7
  (63 shorter events, 35.9 us)
Async XLA Ops:
  7.2 213.6 %copy-start = (f32[16]{0:T(128)S(1)}, f32[16]{0:T(128)}, u32[]{:S(2)}) copy-start(f32[16]{0:T(128)} %param.14) | copy-start | bytes 196
  7.2 7.9 %copy-start.5 = (f32[2,128,1024]{2,1,0:T(8,128)S(1)}, f32[2,128,1024]{2,1,0:T(8,128)}, u32[]{:S(2)}) copy-start(f32[2,128,1024]{2,1,0:T(8,128)} %param.10) | copy-start | bytes 3145732
  7.2 7.9 %copy-start.6 = (f32[2,128,1024]{2,1,0:T(8,128)S(1)}, f32[2,128,1024]{2,1,0:T(8,128)}, u32[]{:S(2)}) copy-start(f32[2,128,1024]{2,1,0:T(8,128)} %param.9) | copy-start | bytes 3145732
  7.2 103.8 %all-gather.3.cloned.1.call-start = ((), (), s32[]{:S(2)}) async-start(), calls=%async_computation.5 | async-start | bytes 2621440 | tf_op jit(solution)/shard_map/all_gather | solution.py:138
  39.8 12.7 %copy-start.1 = (f32[1024,1024,1]{1,0,2:T(8,128)S(1)}, f32[1024,1024,1]{1,0,2:T(8,128)}, u32[]{:S(2)}) copy-start(f32[1024,1024,1]{1,0,2:T(8,128)} %constant.32) | copy-start | bytes 12582916
  64.8 48.7 %copy-start.9 = (f32[128,1024]{1,0:T(8,128)S(1)}, f32[128,1024]{1,0:T(8,128)}, u32[]{:S(2)}) copy-start(f32[128,1024]{1,0:T(8,128)} %param.15) | copy-start | bytes 1572868
  89.2 179.1 %reduce-scatter.2.cloned.1.call-start = ((), (), s32[]{:S(2)}) async-start(), calls=%async_computation.6 | async-start | bytes 1310720 | tf_op jit(solution)/shard_map/reduce_scatter | solution.py:154
  113.5 18.6 %copy-start.10 = (f32[16]{0:T(128)S(1)}, f32[16]{0:T(128)}, u32[]{:S(2)}) copy-start(f32[16]{0:T(128)} %param.13) | copy-start | bytes 196
  214.6 6.2 %copy-start.4 = (f32[2,16,128,1024]{3,2,1,0:T(8,128)}, f32[2,16,128,1024]{3,2,1,0:T(8,128)S(1)}, u32[]{:S(2)}) copy-start(f32[2,16,128,1024]{3,2,1,0:T(8,128)S(1)} %fusion.2) | copy-start | bytes 50331652
  220.8 22.7 %copy-start.7 = (f32[2,2,128,1024]{2,3,1,0:T(8,128)S(1)}, f32[2,2,128,1024]{2,3,1,0:T(8,128)}, u32[]{:S(2)}) copy-start(f32[2,2,128,1024]{2,3,1,0:T(8,128)} %all-gather.3.cloned.1.call-done) | copy-start | bytes 6291460
  243.4 139.7 %all-gather.5.cloned.1.call-start = ((), (), s32[]{:S(2)}) async-start(), calls=%async_computation.7 | async-start | bytes 2621440 | tf_op jit(solution)/shard_map/all_gather | solution.py:138
  290.1 12.7 %copy-start.2 = (f32[1024,1024,1]{1,0,2:T(8,128)S(1)}, f32[1024,1024,1]{1,0,2:T(8,128)}, u32[]{:S(2)}) copy-start(f32[1024,1024,1]{1,0,2:T(8,128)} %constant.32) | copy-start | bytes 12582916
  383.1 12.4 %copy-start.3 = (f32[1024,1024,1]{1,0,2:T(8,128)S(1)}, f32[1024,1024,1]{1,0,2:T(8,128)}, u32[]{:S(2)}) copy-start(f32[1024,1024,1]{1,0,2:T(8,128)} %constant.32) | copy-start | bytes 12582916
  383.1 12.4 %copy-start.8 = (f32[2,2,128,1024]{3,2,0,1:T(8,128)S(1)}, f32[2,2,128,1024]{3,2,0,1:T(8,128)}, u32[]{:S(2)}) copy-start(f32[2,2,128,1024]{3,2,0,1:T(8,128)} %all-gather.5.cloned.1.call-done) | copy-start | bytes 6291460
Sparse Core Ops, SparseCore 0:
  89.3 21.6 all-gather.2
  243.5 24.8 reduce-scatter.1
  345.7 20.6 all-gather.4
where the time goes:
time: 416 us; the launch traced here: 411 us
  other arithmetic  149 us (36%)
  matrix products  89.2 us (21%)
  blocking collectives  76.7 us (18%)
  waiting for transfers between devices  45.6 us (11%)
  local copies, waits for them, and re-layouts  36 us (9%)
  between operations  14.3 us (3%)
    dot_general x8, matrix products, product_of(): return jnp.einsum('mn,fnk->fmk', table, values, precision=HIGHEST)  42.5 us
    all_to_all x2, blocking collectives, row_mix(): lax.all_to_all(section, 'space', split_axis=3, concat_axis=2, tiled=True)  41.3 us
    sub x2, other arithmetic, derivative(): -DEPHASE * spin_real + gradient * spin_imag  38.9 us
    sub x2, other arithmetic, derivative(): -GAMMA * optical_real + doppler * optical_imag - probe_imag  36.8 us
    all_to_all x2, blocking collectives, row_mix(): lax.all_to_all(blended, 'space', split_axis=2, concat_axis=3, tiled=True)  35.4 us
    add x1, other arithmetic, midpoint(): half_optical = optical + 0.5 * DT * rate_optical  33.9 us
    dot_general x8, matrix products, product_of(): return jnp.einsum('fmn,nk->fmk', values, table, precision=HIGHEST)  30 us
    add x2, other arithmetic, midpoint(): return (optical + DT * rate_optical, spin_part + DT * rate_spin)  29.1 us
  transfers between devices with their start and end apart: 3, of which 2 were waited for; matrix products, arithmetic and copies ran while one was open for 9% of the time, Pallas kernels for 0%

commit v1 on v0

--- a/solution.py
+++ b/solution.py
@@ -132,7 +132,12 @@
             full_imag,
             lax.all_to_all(section, "space", split_axis=3, concat_axis=2, tiled=True),
         )
-        return lax.all_to_all(blended, "space", split_axis=2, concat_axis=3, tiled=True)
+        return jnp.concatenate(
+            lax.all_to_all(
+                jnp.stack(jnp.split(blended, lax.axis_size("space"), axis=2)), "space", 0, 0
+            ),
+            axis=3,
+        )
 
     def spread(section):
         return lax.all_gather(section, "vel", axis=3, tiled=True)

time: 416 us -> 399 us (0.959)
  local copies, waits for them, and re-layouts: 36 us -> 16.8 us
  matrix products: 89.2 us -> 97.7 us
  other arithmetic: 149 us -> 143 us
    unnamed x26 -> x24, local copies, waits for them, and re-layouts: 15.7 us -> 6.22 us
    dot_general x8, matrix products: 42.5 us -> 51 us  [product_of(): return jnp.einsum('mn,fnk->fmk', table, values, precision=HIGHEST)]
    all_to_all x4 -> x0, local copies, waits for them, and re-layouts: 7.43 us -> none  [row_mix(): lax.all_to_all(blended, 'space', split_axis=2, concat_axis=3, tiled=True)]
    all_to_all x2 -> x0, other arithmetic: 4.84 us -> none  [row_mix(): lax.all_to_all(blended, 'space', split_axis=2, concat_axis=3, tiled=True)]
    another operation x2 -> x0, local copies, waits for them, and re-layouts: 4.17 us -> none  [mix_left(): jnp.stack([product_of(table_real, real_in) - product_of(table_imag, imag_...]
  transfers between devices with their start and end apart: 3 -> 3, of which waited for: 2 -> 2; matrix products, arithmetic and copies ran while one was open for 9% -> 10% of each run, Pallas kernels for 0% -> 0%
where the time goes in v1:
time: 399 us; the launch traced here: 394 us
  other arithmetic  143 us (36%)
  matrix products  97.7 us (24%)
  blocking collectives  76.3 us (19%)
  waiting for transfers between devices  45.6 us (11%)
  local copies, waits for them, and re-layouts  16.8 us (4%)
  between operations  14.4 us (4%)
    dot_general x8, matrix products, product_of(): return jnp.einsum('mn,fnk->fmk', table, values, precision=HIGHEST)  51 us
    all_to_all x2, blocking collectives, row_mix(): lax.all_to_all(section, 'space', split_axis=3, concat_axis=2, tiled=True)  41.3 us
    sub x2, other arithmetic, derivative(): -DEPHASE * spin_real + gradient * spin_imag  38.4 us
    sub x2, other arithmetic, derivative(): -GAMMA * optical_real + doppler * optical_imag - probe_imag  36.7 us
    all_to_all x2, blocking collectives, row_mix(): lax.all_to_all(jnp.stack(jnp.split(blended, lax.axis_size('space'), axis=...  35.1 us
    add x1, other arithmetic, midpoint(): half_optical = optical + 0.5 * DT * rate_optical  33.9 us
    dot_general x8, matrix products, product_of(): return jnp.einsum('fmn,nk->fmk', values, table, precision=HIGHEST)  30 us
    add x2, other arithmetic, midpoint(): return (optical + DT * rate_optical, spin_part + DT * rate_spin)  29.1 us
  transfers between devices with their start and end apart: 3, of which 2 were waited for; matrix products, arithmetic and copies ran while one was open for 10% of the time, Pallas kernels for 0%

profile of v1, /device:TPU:0, one launch (start us, length us, event | category | flops | bytes accessed | tf_op | source)
XLA Modules:
  0.0 394.2 jit_solution(4723277360425857515)
XLA Ops:
  7.3 2.7 fusion.24
  10.0 2.6 fusion.26
  12.5 2.6 fusion.12
  15.1 2.3 fusion.13
  17.8 21.6 %all_to_all.46 = f32[2,2,128,256]{2,0,1,3:T(2,128)S(1)} all-to-all(f32[2,2,128,256]{2,0,1,3:T(2,128)S(1)} %copy.24), channel_id=1, replica_groups=mesh['space'=8,'vel'=4] {'space'}, dimensions={3} | all-to-all | bytes 1048576 | tf_op jit(solution)/shard_map/all_to_all | solution.py:133
  39.9 6.4 %fusion.34 = f32[2,32,1024]{2,1,0:T(8,128)S(1)} fusion(f32[1024,1024,1]{1,0,2:T(8,128)} %constant.31, f32[2,2,1024,32]{2,3,0,1:T(8,128)S(1)} %all_to_all.35), kind=kOutput, calls=%fused_computation.100 | convolution fusion | flops 805306368 | bytes 4718592 | tf_op jit(solution)/shard_map/mn,fnk->fmk/dot_general | solution.py:39
  46.3 6.3 %fusion.35 = f32[2,32,1024]{2,1,0:T(8,128)S(1)} fusion(f32[1024,1024,1]{1,0,2:T(8,128)} %constant.31, f32[2,2,1024,32]{2,3,0,1:T(8,128)S(1)} %all_to_all.35), kind=kOutput, calls=%fused_computation.101 | convolution fusion | flops 805306368 | bytes 4718592 | tf_op jit(solution)/shard_map/mn,fnk->fmk/dot_general | solution.py:39
  52.5 4.1 %fusion.11 = f32[2,1,1024,32]{2,3,0,1:T(8,128)S(1)} fusion(f32[2,32,1024]{2,1,0:T(8,128)S(1)} %fusion.34, f32[1024,1024,1]{1,0,2:T(8,128)S(1)} %copy-done.1, f32[2,2,1024,32]{2,3,0,1:T(8,128)S(1)} %all_to_all.35), kind=kOutput, calls=%fused_computation.33 | convolution fusion | flops 805371904 | bytes 4980736 | tf_op jit(solution)/shard_map/mn,fnk->fmk/dot_general | solution.py:39
  56.6 13.2 %fusion.10 = f32[2,1,1024,32]{2,3,0,1:T(8,128)S(1)} fusion(f32[2,32,1024]{2,1,0:T(8,128)S(1)} %fusion.35, f32[1024,1024,1]{1,0,2:T(8,128)S(1)} %copy-done.1, f32[2,2,1024,32]{2,3,0,1:T(8,128)S(1)} %all_to_all.35), kind=kOutput, calls=%fused_computation.31 | convolution fusion | flops 805371904 | bytes 4980736 | tf_op jit(solution)/shard_map/mn,fnk->fmk/dot_general | solution.py:39
  70.0 17.5 %all_to_all.47 = f32[8,2,2,128,32]{3,4,1,2,0:T(8,128)S(1)} all-to-all(f32[8,2,2,128,32]{3,4,1,2,0:T(8,128)S(1)} %fusion.87), channel_id=1, replica_groups=mesh['space'=8,'vel'=4] {'space'}, dimensions={0} | all-to-all | bytes 1048576 | tf_op jit(solution)/shard_map/all_to_all | solution.py:136
  88.4 21.7 %all-gather.3.cloned.1.call-done = f32[2,2,128,1024]{2,3,1,0:T(8,128)} async-done(((f32[2,2,128,256]{2,3,1,0:T(8,128)}), f32[2,2,128,1024]{2,3,1,0:T(8,128)}) %all-gather.3.cloned.1.call-update) | async-done | bytes 2097168 | tf_op jit(solution)/shard_map/all_gather | solution.py:143
  112.7 18.4 %subtract_subtract_fusion.1 = (f32[1,16,128,1024]{3,2,1,0:T(8,128)}, f32[1,16,128,1024]{3,2,1,0:T(8,128)}) fusion(f32[2,16,128,1024]{3,2,1,0:T(8,128)} %param.12, f32[2,16,128,1024]{3,2,1,0:T(8,128)} %param.11, f32[128,1024]{1,0:T(8,128)S(1)} %copy-done.9, f32[128,1024]{1,0:T(8,128)S(1)} %copy.30, f32[128,1024]{1,0:T(8,128)S(1)} %copy.29), kind=kLoop, calls=%fused_computation.15 | loop fusion | flops 29360128 | bytes 51904512 | tf_op jit(solution)/shard_map/sub | solution.py:83
  131.1 18.4 %add_subtract_fusion.1 = (f32[1,16,128,1024]{3,2,1,0:T(8,128)}, f32[1,16,128,1024]{3,2,1,0:T(8,128)}) fusion(f32[2,16,128,1024]{3,2,1,0:T(8,128)} %param.12, f32[2,16,128,1024]{3,2,1,0:T(8,128)} %param.11, f32[128,1024]{1,0:T(8,128)S(1)} %copy.30, f32[128,1024]{1,0:T(8,128)S(1)} %copy.29, f32[128,1024]{1,0:T(8,128)S(1)} %copy.28, f32[16]{0:T(128)S(1)} %copy-done.11, ...), kind=kLoop, calls=%fused_computation.17 | loop fusion | flops 33554432 | bytes 52428864 | tf_op jit(solution)/shard_map/sub | solution.py:71
  149.4 33.9 %fusion = (f32[2,16,128,1024]{3,2,1,0:T(8,128)}, f32[2,16,128,1024]{3,2,1,0:T(8,128)}) fusion(f32[2,16,128,1024]{3,2,1,0:T(8,128)} %param.11, f32[1,16,128,1024]{3,2,1,0:T(8,128)} %get-tuple-element.11, f32[1,16,128,1024]{3,2,1,0:T(8,128)} %get-tuple-element.10, f32[2,16,128,1024]{3,2,1,0:T(8,128)} %param.12, f32[1,16,128,1024]{3,2,1,0:T(8,128)} %get-tuple-element.7, ...), kind=kLoop, calls=%fused_computation.1 | loop fusion | flops 25165824 | bytes 100663296 | tf_op jit(solution)/shard_map/add | solution.py:100
  183.3 18.4 %add_subtract_fusion = (f32[1,16,128,1024]{3,2,1,0:T(8,128)}, f32[1,16,128,1024]{3,2,1,0:T(8,128)}) fusion(f32[2,16,128,1024]{3,2,1,0:T(8,128)} %get-tuple-element.23, f32[2,16,128,1024]{3,2,1,0:T(8,128)} %get-tuple-element.22, f32[128,1024]{1,0:T(8,128)S(1)} %copy.30, f32[128,1024]{1,0:T(8,128)S(1)} %copy.29, f32[128,1024]{1,0:T(8,128)S(1)} %copy.28, ...), kind=kLoop, calls=%fused_computation.13 | loop fusion | flops 33554432 | bytes 52428864 | tf_op jit(solution)/shard_map/sub | solution.py:71
  201.7 11.9 %fusion.2 = f32[2,16,128,1024]{3,2,1,0:T(8,128)S(1)} fusion(f32[2,16,128,1024]{3,2,1,0:T(8,128)} %param.11, f32[1,16,128,1024]{3,2,1,0:T(8,128)} %get-tuple-element.9, f32[1,16,128,1024]{3,2,1,0:T(8,128)} %get-tuple-element.8), kind=kLoop, calls=%fused_computation.5 | loop fusion | flops 12582912 | bytes 50331648 | tf_op jit(solution)/shard_map/add | solution.py:105
  213.6 6.2 %copy-done.4 = f32[2,16,128,1024]{3,2,1,0:T(8,128)} copy-done((f32[2,16,128,1024]{3,2,1,0:T(8,128)}, f32[2,16,128,1024]{3,2,1,0:T(8,128)S(1)}, u32[]{:S(2)}) %copy-start.4) | copy-done | bytes 16777240
  219.7 16.7 %fusion.4 = f32[1,2,128,1024]{3,0,2,1:T(1,128)} fusion(f32[2,16,128,1024]{3,2,1,0:T(8,128)S(1)} %fusion.2, f32[16]{0:T(128)S(1)} %copy-done), kind=kOutput, calls=%fused_computation.8 | convolution fusion | flops 50331648 | bytes 17825856 | tf_op jit(solution)/shard_map/cvrn,v->crn/dot_general | solution.py:158
  236.5 3.6 copy.39
  243.5 23.8 %reduce-scatter.2.cloned.1.call-done = f32[2,128,256]{1,2,0:T(8,128)} async-done(((f32[2,128,1024]{1,2,0:T(8,128)}), f32[2,128,256]{1,2,0:T(8,128)}) %reduce-scatter.2.cloned.1.call-update) | async-done | bytes 262160 | tf_op jit(solution)/shard_map/reduce_scatter | solution.py:159
  268.9 19.7 %all_to_all.48 = f32[2,2,128,256]{2,1,0,3:T(2,128)S(1)} all-to-all(f32[2,2,128,256]{2,1,0,3:T(2,128)S(1)} %copy.32), channel_id=1, replica_groups=mesh['space'=8,'vel'=4] {'space'}, dimensions={3} | all-to-all | bytes 1048576 | tf_op jit(solution)/shard_map/all_to_all | solution.py:133
  289.1 6.4 %fusion.36 = f32[2,32,1024]{2,1,0:T(8,128)S(1)} fusion(f32[1024,1024,1]{1,0,2:T(8,128)} %constant.31, f32[2,2,1024,32]{2,3,0,1:T(8,128)S(1)} %all_to_all.40), kind=kOutput, calls=%fused_computation.102 | convolution fusion | flops 805306368 | bytes 4718592 | tf_op jit(solution)/shard_map/mn,fnk->fmk/dot_general | solution.py:39
  295.5 6.3 %fusion.37 = f32[2,32,1024]{2,1,0:T(8,128)S(1)} fusion(f32[1024,1024,1]{1,0,2:T(8,128)} %constant.31, f32[2,2,1024,32]{2,3,0,1:T(8,128)S(1)} %all_to_all.40), kind=kOutput, calls=%fused_computation.103 | convolution fusion | flops 805306368 | bytes 4718592 | tf_op jit(solution)/shard_map/mn,fnk->fmk/dot_general | solution.py:39
  301.7 4.1 %fusion.9 = f32[2,1,1024,32]{2,3,0,1:T(8,128)S(1)} fusion(f32[2,32,1024]{2,1,0:T(8,128)S(1)} %fusion.36, f32[1024,1024,1]{1,0,2:T(8,128)S(1)} %copy-done.2, f32[2,2,1024,32]{2,3,0,1:T(8,128)S(1)} %all_to_all.40), kind=kOutput, calls=%fused_computation.29 | convolution fusion | flops 805371904 | bytes 4980736 | tf_op jit(solution)/shard_map/mn,fnk->fmk/dot_general | solution.py:39
  305.8 4.3 %fusion.8 = f32[2,1,1024,32]{2,3,0,1:T(8,128)S(1)} fusion(f32[2,32,1024]{2,1,0:T(8,128)S(1)} %fusion.37, f32[1024,1024,1]{1,0,2:T(8,128)S(1)} %copy-done.2, f32[2,2,1024,32]{2,3,0,1:T(8,128)S(1)} %all_to_all.40), kind=kOutput, calls=%fused_computation.27 | convolution fusion | flops 805371904 | bytes 4980736 | tf_op jit(solution)/shard_map/mn,fnk->fmk/dot_general | solution.py:39
  310.3 17.5 %all_to_all.49 = f32[8,2,2,128,32]{3,4,1,2,0:T(8,128)S(1)} all-to-all(f32[8,2,2,128,32]{3,4,1,2,0:T(8,128)S(1)} %fusion.85), channel_id=1, replica_groups=mesh['space'=8,'vel'=4] {'space'}, dimensions={0} | all-to-all | bytes 1048576 | tf_op jit(solution)/shard_map/all_to_all | solution.py:136
  328.9 20.0 %subtract_subtract_fusion = (f32[1,16,128,1024]{3,2,1,0:T(8,128)}, f32[1,16,128,1024]{3,2,1,0:T(8,128)}) fusion(f32[2,16,128,1024]{3,2,1,0:T(8,128)} %get-tuple-element.23, f32[2,16,128,1024]{3,2,1,0:T(8,128)} %get-tuple-element.22, f32[128,1024]{1,0:T(8,128)S(1)} %copy-done.10, f32[128,1024]{1,0:T(8,128)S(1)} %copy.30, f32[128,1024]{1,0:T(8,128)S(1)} %copy.29), kind=kLoop, calls=%fused_computation.11 | loop fusion | flops 29360128 | bytes 51904512 | tf_op jit(solution)/shard_map/sub | solution.py:83
  348.9 17.2 %fusion.3 = f32[2,16,128,1024]{3,2,1,0:T(8,128)} fusion(f32[2,16,128,1024]{3,2,1,0:T(8,128)} %param.12, f32[1,16,128,1024]{3,2,1,0:T(8,128)} %get-tuple-element.5, f32[1,16,128,1024]{3,2,1,0:T(8,128)} %get-tuple-element.4), kind=kLoop, calls=%fused_computation.7 | loop fusion | flops 12582912 | bytes 50331648 | tf_op jit(solution)/shard_map/add | solution.py:105
  366.1 6.2 %fusion.31 = f32[2,128,1024]{2,1,0:T(8,128)S(1)} fusion(f32[1024,1024,1]{1,0,2:T(8,128)} %constant.31, f32[2,2,128,1024]{3,2,0,1:T(8,128)} %all-gather.5.cloned.1.call-done), kind=kOutput, calls=%fused_computation.88 | convolution fusion | flops 3221225472 | bytes 6291456 | tf_op jit(solution)/shard_map/fmn,nk->fmk/dot_general | solution.py:54
  372.3 6.2 %fusion.30 = f32[2,128,1024]{2,1,0:T(8,128)S(1)} fusion(f32[1024,1024,1]{1,0,2:T(8,128)} %constant.31, f32[2,2,128,1024]{3,2,0,1:T(8,128)} %all-gather.5.cloned.1.call-done), kind=kOutput, calls=%fused_computation.87 | convolution fusion | flops 3221225472 | bytes 6291456 | tf_op jit(solution)/shard_map/fmn,nk->fmk/dot_general | solution.py:54
  378.5 3.7 fusion.6
  382.3 3.7 fusion.7
  (70 shorter events, 12.4 us)
Async XLA Ops:
  7.2 212.6 %copy-start = (f32[16]{0:T(128)S(1)}, f32[16]{0:T(128)}, u32[]{:S(2)}) copy-start(f32[16]{0:T(128)} %param.14) | copy-start | bytes 196
  7.2 7.9 %copy-start.5 = (f32[2,128,1024]{2,1,0:T(8,128)S(1)}, f32[2,128,1024]{2,1,0:T(8,128)}, u32[]{:S(2)}) copy-start(f32[2,128,1024]{2,1,0:T(8,128)} %param.10) | copy-start | bytes 3145732
  7.2 7.9 %copy-start.6 = (f32[2,128,1024]{2,1,0:T(8,128)S(1)}, f32[2,128,1024]{2,1,0:T(8,128)}, u32[]{:S(2)}) copy-start(f32[2,128,1024]{2,1,0:T(8,128)} %param.9) | copy-start | bytes 3145732
  7.2 103.0 %all-gather.3.cloned.1.call-start = ((), (), s32[]{:S(2)}) async-start(), calls=%async_computation.5 | async-start | bytes 2621440 | tf_op jit(solution)/shard_map/all_gather | solution.py:143
  39.8 12.7 %copy-start.1 = (f32[1024,1024,1]{1,0,2:T(8,128)S(1)}, f32[1024,1024,1]{1,0,2:T(8,128)}, u32[]{:S(2)}) copy-start(f32[1024,1024,1]{1,0,2:T(8,128)} %constant.32) | copy-start | bytes 12582916
  69.8 42.8 %copy-start.9 = (f32[128,1024]{1,0:T(8,128)S(1)}, f32[128,1024]{1,0:T(8,128)}, u32[]{:S(2)}) copy-start(f32[128,1024]{1,0:T(8,128)} %param.15) | copy-start | bytes 1572868
  88.4 179.0 %reduce-scatter.2.cloned.1.call-start = ((), (), s32[]{:S(2)}) async-start(), calls=%async_computation.6 | async-start | bytes 1310720 | tf_op jit(solution)/shard_map/reduce_scatter | solution.py:159
  112.7 18.4 %copy-start.11 = (f32[16]{0:T(128)S(1)}, f32[16]{0:T(128)}, u32[]{:S(2)}) copy-start(f32[16]{0:T(128)} %param.13) | copy-start | bytes 196
  213.6 6.2 %copy-start.4 = (f32[2,16,128,1024]{3,2,1,0:T(8,128)}, f32[2,16,128,1024]{3,2,1,0:T(8,128)S(1)}, u32[]{:S(2)}) copy-start(f32[2,16,128,1024]{3,2,1,0:T(8,128)S(1)} %fusion.2) | copy-start | bytes 50331652
  219.7 22.7 %copy-start.7 = (f32[2,2,128,1024]{2,3,1,0:T(8,128)S(1)}, f32[2,2,128,1024]{2,3,1,0:T(8,128)}, u32[]{:S(2)}) copy-start(f32[2,2,128,1024]{2,3,1,0:T(8,128)} %all-gather.3.cloned.1.call-done) | copy-start | bytes 6291460
  242.3 123.8 %all-gather.5.cloned.1.call-start = ((), (), s32[]{:S(2)}) async-start(), calls=%async_computation.7 | async-start | bytes 2621440 | tf_op jit(solution)/shard_map/all_gather | solution.py:143
  289.0 12.7 %copy-start.2 = (f32[1024,1024,1]{1,0,2:T(8,128)S(1)}, f32[1024,1024,1]{1,0,2:T(8,128)}, u32[]{:S(2)}) copy-start(f32[1024,1024,1]{1,0,2:T(8,128)} %constant.32) | copy-start | bytes 12582916
  301.7 27.2 %copy-start.10 = (f32[128,1024]{1,0:T(8,128)S(1)}, f32[128,1024]{1,0:T(8,128)}, u32[]{:S(2)}) copy-start(f32[128,1024]{1,0:T(8,128)} %param.15) | copy-start | bytes 1572868
  366.1 12.4 %copy-start.3 = (f32[1024,1024,1]{1,0,2:T(8,128)S(1)}, f32[1024,1024,1]{1,0,2:T(8,128)}, u32[]{:S(2)}) copy-start(f32[1024,1024,1]{1,0,2:T(8,128)} %constant.32) | copy-start | bytes 12582916
  366.1 12.4 %copy-start.8 = (f32[2,2,128,1024]{3,2,0,1:T(8,128)S(1)}, f32[2,2,128,1024]{3,2,0,1:T(8,128)}, u32[]{:S(2)}) copy-start(f32[2,2,128,1024]{3,2,0,1:T(8,128)} %all-gather.5.cloned.1.call-done) | copy-start | bytes 6291460
Sparse Core Ops, SparseCore 0:
  88.5 21.6 all-gather.2
  242.5 24.8 reduce-scatter.1
  329.0 20.6 all-gather.4
